TPU v7x, 32 devices: a whole 2x2x4 slice. The times are simulated.
32 devices in a mesh: task: 4 (over z), shard: 2 (over y), rep: 4 (over x, core).
Axes of the slice: x: 2, y: 2, z: 4, core: 2. Of those that a mesh axis runs over, the one named last changes fastest.
Arguments:
- deltas: bfloat16 [8, 32, 16, 8192], P('task', None, None, ('shard', 'rep')), may hold values from -4 to 4
- base: bfloat16 [32, 16, 2, 4096], P(('task', 'shard'), None, None, 'rep'), may hold values from -60 to 60
- sel_index: int32 [8, 8], replicated, may hold values from 0 to 31, as said below
- sel_count: int32 [8], replicated, may hold values from 1 to 8
- scale_num: int32 [8], replicated, may hold values from 1 to 12
Outputs:
- merged: bfloat16 [32, 16, 8192], P(('task', 'shard'))
Inputs may be any that keep to these rules, and one draw needn't show every extreme that they name: `sel_index`: for task i the first sel_count[i] entries are distinct and ascending; at most 1 of them lie in any aligned group of 4 blocks, and in every draw some group holds 1 selected blocks of every task, and some task selects 1 block in every group. Later entries are block numbers that are not selected.
All inputs are finite; a program needn't handle non-finite values.
Results may differ from a plain program's by a relative error of at most 0.00045.
Values may be sent and summed in bfloat16 or wider, within the bound.
A program may use at most 64 MiB of HBM per device.

v0:
```python
import jax
import jax.numpy as jnp
from jax import lax
from jax.sharding import PartitionSpec as P

LAYERS = 4


denominator = 8.0
epsilon = 1e-06


def slot_tables(sel_index, sel_count, own_blocks, owners):
    entries = jnp.arange(sel_index.shape[1], dtype=jnp.int32)
    valid = entries[None, :] < sel_count[:, None]
    owner_of = sel_index // own_blocks
    owner_ids = jnp.arange(owners, dtype=jnp.int32)
    earlier = valid[:, :, None] & (owner_of[:, :, None] < owner_ids[None, None, :])
    within = valid[:, :, None] & (owner_of[:, :, None] == owner_ids[None, None, :])
    before = jnp.sum(earlier.astype(jnp.int32), axis=1)
    inside = jnp.sum(within.astype(jnp.int32), axis=1)
    return (before, inside)


def slot_blocks(sel_index, start, capacity):
    limit = sel_index.shape[1] - 1
    where_at = jnp.minimum(
        start[:, :, None] + jnp.arange(capacity, dtype=jnp.int32)[None, None, :], limit
    )
    flat = jnp.take_along_axis(sel_index, where_at.reshape(sel_index.shape[0], -1), axis=1)
    return flat.reshape(where_at.shape)


def layer_sums(values, onehot):
    per_block = jnp.sum(values * values, axis=(1, 2, 3))
    return jnp.sum(per_block[:, None] * onehot, axis=0)


def shards(deltas, base, sel_index, sel_count, scale_num):
    task_dev = deltas.shape[0]
    nb_all = deltas.shape[1]
    rows = deltas.shape[2]
    width = deltas.shape[3]
    n_task = lax.axis_size("task")
    n_shard = lax.axis_size("shard")
    owners = n_task * n_shard
    own_blocks = base.shape[0]
    capacity = own_blocks // 4
    my_task = lax.axis_index("task")
    owner_me = my_task * n_shard + lax.axis_index("shard")
    before, inside = slot_tables(sel_index, sel_count, own_blocks, owners)
    base_wide = base.astype(jnp.float32)
    layer_span = nb_all // LAYERS
    layer_of = (owner_me * own_blocks + jnp.arange(own_blocks, dtype=jnp.int32)) // layer_span
    onehot = (layer_of[:, None] == jnp.arange(LAYERS, dtype=jnp.int32)[None, :]).astype(jnp.float32)
    base_sq = layer_sums(base_wide, onehot)
    first = my_task * task_dev
    mine_index = lax.dynamic_slice_in_dim(sel_index, first, task_dev, 0)
    mine_before = lax.dynamic_slice_in_dim(before, first, task_dev, 0)
    mine_inside = lax.dynamic_slice_in_dim(inside, first, task_dev, 0)
    chosen = jnp.transpose(slot_blocks(mine_index, mine_before, capacity), (1, 0, 2))
    live = jnp.transpose(
        jnp.arange(capacity, dtype=jnp.int32)[None, None, :] < mine_inside[:, :, None], (1, 0, 2)
    )
    holder = jnp.broadcast_to(jnp.arange(task_dev, dtype=jnp.int32)[None, :, None], chosen.shape)
    outgoing = deltas[holder, chosen]
    outgoing = jnp.where(live[:, :, :, None, None], outgoing, jnp.zeros((), jnp.bfloat16))
    outgoing = outgoing.reshape(n_task, n_shard, task_dev, capacity, rows, width)
    flat_out = outgoing.reshape(owners, task_dev, capacity, rows, width)
    incoming = lax.all_to_all(flat_out, ("task", "shard"), split_axis=0, concat_axis=0, tiled=True)
    incoming = incoming.reshape(n_task, n_shard, task_dev, capacity, rows, width)
    start_me = lax.dynamic_slice_in_dim(before, owner_me, 1, 1)
    count_me = lax.dynamic_slice_in_dim(inside, owner_me, 1, 1)
    arrived = slot_blocks(sel_index, start_me, capacity)[:, 0, :]
    arrived_live = jnp.arange(capacity, dtype=jnp.int32)[None, :] < count_me
    local_block = arrived - owner_me * own_blocks
    factor = scale_num.astype(jnp.float32) / denominator
    match = (
        local_block[None, :, :] == jnp.arange(own_blocks, dtype=jnp.int32)[:, None, None]
    ) & arrived_live[None, :, :]
    weight = jnp.where(match, factor[None, :, None], 0.0)
    weight = weight.reshape(own_blocks, n_task, task_dev, capacity).astype(jnp.bfloat16)
    combined = jnp.einsum("jtak,tsakrc->jrsc", weight, incoming, preferred_element_type=jnp.float32)
    merged_raw = base_wide + combined
    merged_sq = layer_sums(merged_raw, onehot)
    base_total, merged_total = lax.psum((base_sq, merged_sq), ("task", "shard", "rep"))
    ratio = jnp.sqrt((base_total + epsilon) / (merged_total + epsilon))
    block_ratio = jnp.sum(onehot * ratio[None, :], axis=1)
    result = (merged_raw * block_ratio[:, None, None, None]).astype(jnp.bfloat16)
    copies = lax.all_gather(result, "rep", axis=3, tiled=True)
    return copies.reshape(own_blocks, rows, -1)


def solution(mesh):
    placed = (
        P("task", None, None, ("shard", "rep")),
        P(("task", "shard"), None, None, "rep"),
        P(),
        P(),
        P(),
    )
    return jax.shard_map(
        shards,
        mesh=mesh,
        in_specs=placed,
        out_specs=P(("task", "shard"), None, None),
        check_vma=False,
    )
```

profile of v0, /device:TPU:9, one launch (start us, length us, event | category | flops | bytes accessed | tf_op | source)
XLA Modules:
  0.0 100.4 jit_solution(3210232870957093238)
XLA Ops:
  6.5 0.0 copy-start
  6.5 0.9 iota_compare_fusion.3
  7.4 0.7 add_select_fusion
  8.1 0.7 constant_dynamic-slice_fusion
  8.8 0.1 convert_reduce_fusion.1
  8.9 0.1 copy.47
  9.0 0.1 reshape.196
  9.1 0.0 copy-start.3
  9.1 0.0 copy-start.1
  9.1 0.7 gather_fusion.1
  9.8 0.0 copy-start.2
  9.8 0.1 reshape.199
  9.9 0.1 copy.51
  10.0 0.1 reshape.190
  10.1 0.0 copy-done
  10.1 0.6 gather_fusion
  10.7 0.9 broadcast_select_fusion
  11.6 5.7 %all-to-all-start = ((bf16[8,2,1,16,1024]{4,3,1,2,0:T(8,128)(2,1)}), bf16[8,2,1,16,1024]{4,3,1,2,0:T(8,128)(2,1)S(1)}, u32[]{:S(2)}, u32[]{:S(2)}) async-start(bf16[8,2,1,16,1024]{4,3,1,2,0:T(8,128)(2,1)} %broadcast_select_fusion), calls=%async_computation | async-start | bytes 1048576 | tf_op jit(solution)/shard_map/all_to_all | solution.py:70
  17.3 0.0 all-gather.2.cloned.1.call-start
  17.3 0.0 copy-done.3
  17.4 0.1 broadcast_in_dim.33
  17.4 0.1 copy.57
  17.6 0.2 fusion.8
  17.7 0.1 and.70
  17.8 0.1 copy.56
  17.9 0.2 fusion.9
  18.2 0.1 copy.64
  18.2 0.1 copy.65
  18.3 0.1 or_reduce_fusion
  18.4 0.0 copy-done.1
  18.5 0.6 gather_fusion.2
  19.1 0.1 copy.54
  19.2 0.2 subtract_reduce_fusion
  19.4 0.1 eq.52
  19.4 0.1 copy.55
  19.6 0.0 copy-done.2
  19.6 0.4 fusion.1
  20.0 8.5 %all-to-all-done = bf16[8,2,1,16,1024]{4,3,1,2,0:T(8,128)(2,1)S(1)} async-done(((bf16[8,2,1,16,1024]{4,3,1,2,0:T(8,128)(2,1)}), bf16[8,2,1,16,1024]{4,3,1,2,0:T(8,128)(2,1)S(1)}, u32[]{:S(2)}, u32[]{:S(2)}) %all-to-all-start) | async-done | bytes 524320 | tf_op jit(solution)/shard_map/all_to_all | solution.py:70
  28.4 1.0 multiply_reduce_fusion
  29.4 0.1 select_reduce_fusion.2
  29.5 41.8 %all-reduce = (f32[4]{0:T(128)S(1)}, f32[4]{0:T(128)S(1)}) all-reduce(f32[4]{0:T(128)S(1)} %get-tuple-element.8, f32[4]{0:T(128)S(1)} %get-tuple-element.7), channel_id=1, replica_groups=mesh['task'=4,'shard'=2,'rep'=4] {'task','shard','rep'}, use_global_device_ids=true, to_apply=%region_7.8 | all-reduce | flops 8 | bytes 64 | tf_op jit(solution)/shard_map/psum | solution.py:86
  71.3 0.2 select_reduce_fusion
  71.4 0.9 multiply_convert_fusion
  72.3 0.0 all-gather.2.cloned.1.call-update
  72.3 17.3 %all-gather.2.cloned.1.call-done = bf16[4,16,2,4096]{3,0,1,2:T(4,128)(2,1)} async-done(((bf16[4,16,2,1024]{3,0,1,2:T(4,128)(2,1)}), bf16[4,16,2,4096]{3,0,1,2:T(4,128)(2,1)}) %all-gather.2.cloned.1.call-update) | async-done | bytes 1048592 | tf_op jit(solution)/shard_map/all_gather | solution.py:90
  89.6 2.3 %copy.59 = bf16[4,16,2,4096]{3,2,1,0:T(2,128)(2,1)S(1)} copy(bf16[4,16,2,4096]{3,0,1,2:T(4,128)(2,1)} %all-gather.2.cloned.1.call-done) | data formatting | bytes 2097152 | tf_op jit(solution)/shard_map/all_gather | solution.py:90
  92.0 1.6 %reshape.187 = bf16[4,16,8192]{2,1,0:T(8,128)(2,1)} reshape(bf16[4,16,2,4096]{3,2,1,0:T(2,128)(2,1)S(1)} %copy.59) | data formatting | bytes 2097152 | tf_op jit(solution)/shard_map/reshape | solution.py:91
  (12 shorter events, 0.1 us)
Async XLA Ops:
  6.5 3.6 %copy-start = (bf16[2,32,16,1024]{3,2,1,0:T(8,128)(2,1)S(1)}, bf16[2,32,16,1024]{3,2,1,0:T(8,128)(2,1)}, u32[]{:S(2)}) copy-start(bf16[2,32,16,1024]{3,2,1,0:T(8,128)(2,1)} %param.5) | copy-start | bytes 6291460
  9.1 8.2 %copy-start.3 = (s32[8]{0:T(128)S(1)}, s32[8]{0:T(128)}, u32[]{:S(2)}) copy-start(s32[8]{0:T(128)} %param.9) | copy-start | bytes 100
  9.1 9.3 %copy-start.1 = (s32[8,8]{1,0:T(8,128)S(1)}, s32[8,8]{1,0:T(8,128)}, u32[]{:S(2)}) copy-start(s32[8,8]{1,0:T(8,128)} %param.7) | copy-start | bytes 772
  9.8 9.8 %copy-start.2 = (bf16[4,16,2,1024]{3,2,1,0:T(2,128)(2,1)S(1)}, bf16[4,16,2,1024]{3,2,1,0:T(2,128)(2,1)}, u32[]{:S(2)}) copy-start(bf16[4,16,2,1024]{3,2,1,0:T(2,128)(2,1)} %param.6) | copy-start | bytes 786436
  11.6 16.8 %all-to-all-start = ((bf16[8,2,1,16,1024]{4,3,1,2,0:T(8,128)(2,1)}), bf16[8,2,1,16,1024]{4,3,1,2,0:T(8,128)(2,1)S(1)}, u32[]{:S(2)}, u32[]{:S(2)}) async-start(bf16[8,2,1,16,1024]{4,3,1,2,0:T(8,128)(2,1)} %broadcast_select_fusion), calls=%async_computation | async-start | bytes 1048576 | tf_op jit(solution)/shard_map/all_to_all | solution.py:70
  17.3 72.3 %all-gather.2.cloned.1.call-start = ((), (), s32[]{:S(2)}) async-start(), calls=%async_computation.1 | async-start | bytes 1310720 | tf_op jit(solution)/shard_map/all_gather | solution.py:90
Sparse Core Ops, SparseCore 0:
  72.5 17.1 all-gather.1
where the time goes:
time: 102 us; the launch traced here: 100 us
  blocking collectives  41.8 us (41%)
  waiting for transfers between devices  25.8 us (25%)
  between operations  13.5 us (13%)
  local copies, waits for them, and re-layouts  7.79 us (8%)
  starting transfers between devices  5.72 us (6%)
  other arithmetic  4.87 us (5%)
    psum x1, blocking collectives, shards(): lax.psum((base_sq, merged_sq), ('task', 'shard', 'rep'))  41.8 us
    all_gather x1, waiting for transfers between devices, shards(): copies = lax.all_gather(result, 'rep', axis=3, tiled=True)  17.3 us
    all_to_all x1, waiting for transfers between devices, shards(): lax.all_to_all(flat_out, ('task', 'shard'), split_axis=0, concat_axis=0,...  8.45 us
    all_to_all x1, starting transfers between devices, shards(): lax.all_to_all(flat_out, ('task', 'shard'), split_axis=0, concat_axis=0,...  5.72 us
    all_gather x1, local copies, waits for them, and re-layouts, shards(): copies = lax.all_gather(result, 'rep', axis=3, tiled=True)  2.31 us
  transfers between devices with their start and end apart: 2, of which 2 were waited for; matrix products, arithmetic and copies ran while one was open for 3% of the time, Pallas kernels for 0%

commit v1 on v0

v1 whole, which is shorter than its diff:
```python
import functools

import jax
import jax.numpy as jnp
from jax import lax
from jax.experimental import pallas as pl
from jax.experimental.pallas import tpu as pltpu
from jax.sharding import PartitionSpec as P

LAYERS = 4
LANES = 128
MESH = pl.DeviceIdType.MESH

denominator = 8.0
epsilon = 1e-06


def offset_peers(n_task, n_shard, n_rep, layer_tasks):
    owners = [(a, b) for a in range(n_task) for b in range(n_shard)][1:]
    group = [(a, b, c) for a in range(layer_tasks) for b in range(n_shard) for c in range(n_rep)][1:]
    return owners, group


def kernel(
    dims, index_ref, count_ref, scale_ref, deltas_ref, base_ref, out_ref,
    held, base_held, outgoing, incoming, raw, stat_mine, stat_in,
    load_sems, base_sem, send_sems, recv_sems, stat_send, stat_recv, col_send, col_recv,
):
    n_task, n_shard, n_rep, layer_tasks = dims
    task_dev, nb_all, rows, width = deltas_ref.shape
    groups, own_blocks = raw.shape[:2]
    group_cols = out_ref.shape[2] // groups
    kmax = index_ref.shape[1]
    owner_offsets, stat_offsets = offset_peers(n_task, n_shard, n_rep, layer_tasks)

    my_task = lax.axis_index("task")
    my_shard = lax.axis_index("shard")
    my_rep = lax.axis_index("rep")

    loads = []
    for a in range(task_dev):
        copy = pltpu.make_async_copy(deltas_ref.at[a], held.at[a], load_sems.at[a])
        copy.start()
        loads.append(copy)
    base_copy = pltpu.make_async_copy(base_ref, base_held, base_sem)
    base_copy.start()

    def owner_at(off, sign=1):
        t = lax.rem(my_task + sign * off[0] + n_task, n_task)
        s = lax.rem(my_shard + sign * off[1] + n_shard, n_shard)
        return t, s

    layer_first = (my_task // layer_tasks) * layer_tasks

    def stat_at(off):
        t = layer_first + lax.rem(my_task - layer_first + off[0], layer_tasks)
        s = lax.rem(my_shard + off[1], n_shard)
        r = lax.rem(my_rep + off[2], n_rep)
        return t, s, r

    barrier = pltpu.get_barrier_semaphore()
    for off in owner_offsets:
        t, s = owner_at(off)
        pl.semaphore_signal(barrier, inc=1, device_id=(t, s, my_rep), device_id_type=MESH)
    extra = [o for o in stat_offsets if o[2] != 0 or (o[0] != 0 and n_task % layer_tasks)]
    for off in extra:
        pl.semaphore_signal(barrier, inc=1, device_id=stat_at(off), device_id_type=MESH)

    def block_for(task, owner):
        count = count_ref[task]

        def step(k, carry):
            block, live = carry
            entry = index_ref[task, k]
            hit = (k < count) & (entry // own_blocks == owner)
            return jnp.where(hit, entry, block), jnp.where(hit, 1, live)

        start = (owner * own_blocks, jnp.int32(0))
        return lax.fori_loop(0, kmax, step, start, unroll=kmax <= 8)

    chosen = {}
    for d, off in enumerate([(0, 0)] + owner_offsets):
        t, s = owner_at(off)
        for a in range(task_dev):
            chosen[d, a] = block_for(my_task * task_dev + a, t * n_shard + s)[0]

    for copy in loads:
        copy.wait()

    for d, off in enumerate(owner_offsets):
        for a in range(task_dev):
            outgoing[d, a] = held[a, chosen[d + 1, a]]

    pl.semaphore_wait(barrier, len(owner_offsets) + len(extra))

    sends = []
    for d, off in enumerate(owner_offsets):
        t, s = owner_at(off)
        copy = pltpu.make_async_remote_copy(
            src_ref=outgoing.at[d], dst_ref=incoming.at[d],
            send_sem=send_sems.at[d], recv_sem=recv_sems.at[d],
            device_id=(t, s, my_rep), device_id_type=MESH,
        )
        copy.start()
        sends.append(copy)

    def fold(values):
        total = values[:, 0:LANES]
        for c in range(LANES, values.shape[1], LANES):
            total = total + values[:, c:c + LANES]
        return total

    base_copy.wait()
    base_sum = jnp.zeros((rows, LANES), jnp.float32)
    for g in range(groups):
        for j in range(own_blocks):
            wide = base_held[j, g].astype(jnp.float32)
            raw[g, j] = wide
            base_sum = base_sum + fold(wide * wide)
    stat_mine[0] = base_sum

    my_owner = my_task * n_shard + my_shard

    def add_in(off, pieces):
        t, s = owner_at(off, -1)
        weights = []
        for a in range(task_dev):
            task = t * task_dev + a
            block, live = block_for(task, my_owner)
            factor = scale_ref[task].astype(jnp.float32) / denominator
            factor = jnp.where(live == 1, factor, 0.0)
            local = block - my_owner * own_blocks
            weights.append([jnp.where(local == j, factor, 0.0) for j in range(own_blocks)])
        pieces = [p.astype(jnp.float32) for p in pieces()]
        for j in range(own_blocks):
            total = raw[s, j]
            for a in range(task_dev):
                total = total + weights[a][j] * pieces[a]
            raw[s, j] = total

    add_in((0, 0), lambda: [held[a, chosen[0, a]] for a in range(task_dev)])
    for d, off in enumerate(owner_offsets):
        def pieces(d=d):
            sends[d].wait_recv()
            return [incoming[d, a] for a in range(task_dev)]
        add_in(off, pieces)

    merged_sum = jnp.zeros((rows, LANES), jnp.float32)
    for g in range(groups):
        for j in range(own_blocks):
            value = raw[g, j]
            merged_sum = merged_sum + fold(value * value)
    stat_mine[1] = merged_sum

    stats = []
    for e, off in enumerate(stat_offsets):
        copy = pltpu.make_async_remote_copy(
            src_ref=stat_mine, dst_ref=stat_in.at[e],
            send_sem=stat_send.at[e], recv_sem=stat_recv.at[e],
            device_id=stat_at(off), device_id_type=MESH,
        )
        copy.start()
        stats.append(copy)
    base_total, merged_total = base_sum, merged_sum
    for e in range(len(stat_offsets)):
        stats[e].wait_recv()
        base_total = base_total + stat_in[e, 0]
        merged_total = merged_total + stat_in[e, 1]
    base_total = jnp.sum(base_total, axis=(0, 1), keepdims=True)
    merged_total = jnp.sum(merged_total, axis=(0, 1), keepdims=True)
    ratio = jnp.sqrt((base_total + epsilon) / (merged_total + epsilon))

    cols = []
    for g in range(groups):
        col = pl.multiple_of(g * group_cols + my_rep * width, width)
        for j in range(own_blocks):
            out_ref[j, :, pl.ds(col, width)] = (raw[g, j] * ratio).astype(jnp.bfloat16)
        part = out_ref.at[:, :, pl.ds(col, width)]
        for c in range(1, n_rep):
            copy = pltpu.make_async_remote_copy(
                src_ref=part, dst_ref=part,
                send_sem=col_send.at[g, c - 1], recv_sem=col_recv.at[g, c - 1],
                device_id=(my_task, my_shard, lax.rem(my_rep + c, n_rep)), device_id_type=MESH,
            )
            copy.start()
            cols.append(copy)
    for copy in cols:
        copy.wait_recv()
    for copy in sends + stats + cols:
        copy.wait_send()


def solution(mesh):
    n_task, n_shard, n_rep = mesh.shape["task"], mesh.shape["shard"], mesh.shape["rep"]

    def shards(deltas, base, sel_index, sel_count, scale_num):
        task_dev, nb_all, rows, width = deltas.shape
        own_blocks, _, groups, _ = base.shape
        layer_tasks = nb_all // LAYERS // own_blocks // n_shard
        dims = (n_task, n_shard, n_rep, layer_tasks)
        peers, group = offset_peers(*dims)
        smem = pl.BlockSpec(memory_space=pltpu.SMEM)
        hbm = pl.BlockSpec(memory_space=pl.ANY)
        base = jnp.transpose(base, (0, 2, 1, 3))
        return pl.pallas_call(
            functools.partial(kernel, dims),
            out_shape=jax.ShapeDtypeStruct((own_blocks, rows, groups * n_rep * width), jnp.bfloat16),
            in_specs=[smem, smem, smem, hbm, hbm],
            out_specs=pl.BlockSpec(memory_space=pltpu.VMEM),
            scratch_shapes=[
                pltpu.VMEM(deltas.shape, jnp.bfloat16),
                pltpu.VMEM(base.shape, jnp.bfloat16),
                pltpu.VMEM((len(peers), task_dev, rows, width), jnp.bfloat16),
                pltpu.VMEM((len(peers), task_dev, rows, width), jnp.bfloat16),
                pltpu.VMEM((groups, own_blocks, rows, width), jnp.float32),
                pltpu.VMEM((2, rows, LANES), jnp.float32),
                pltpu.VMEM((len(group), 2, rows, LANES), jnp.float32),
                pltpu.SemaphoreType.DMA((task_dev,)),
                pltpu.SemaphoreType.DMA,
                pltpu.SemaphoreType.DMA((len(peers),)),
                pltpu.SemaphoreType.DMA((len(peers),)),
                pltpu.SemaphoreType.DMA((len(group),)),
                pltpu.SemaphoreType.DMA((len(group),)),
                pltpu.SemaphoreType.DMA((groups, n_rep - 1)),
                pltpu.SemaphoreType.DMA((groups, n_rep - 1)),
            ],
            compiler_params=pltpu.CompilerParams(collective_id=0, has_side_effects=True),
        )(sel_index, sel_count, scale_num, deltas, base)

    placed = (
        P("task", None, None, ("shard", "rep")),
        P(("task", "shard"), None, None, "rep"),
        P(),
        P(),
        P(),
    )
    return jax.shard_map(
        shards,
        mesh=mesh,
        in_specs=placed,
        out_specs=P(("task", "shard"), None, None),
        check_vma=False,
    )
```

time: 102 us -> 40.1 us (0.39); the launches traced: 100 us -> 39.9 us
  blocking collectives: 41.8 us -> 0 us
  Pallas kernels: 0 us -> 35.9 us
  waiting for transfers between devices: 25.8 us -> 0 us
  between operations: 13.5 us -> 0.01 us
  starting transfers between devices: 5.72 us -> 0 us
  other arithmetic: 4.87 us -> 0 us
  local copies, waits for them, and re-layouts: 7.79 us -> 3.97 us
    psum x1 -> x0, blocking collectives: 41.8 us -> none  [shards(): lax.psum((base_sq, merged_sq), ('task', 'shard', 'rep'))]
    pallas_call x0 -> x1, Pallas kernels: none -> 35.9 us  [shards(): pl.pallas_call(functools.partial(kernel, dims), out_shape=jax.ShapeDtypeS...]
    all_gather x1 -> x0, waiting for transfers between devices: 17.3 us -> none  [shards(): copies = lax.all_gather(result, 'rep', axis=3, tiled=True)]
    all_to_all x1 -> x0, waiting for transfers between devices: 8.45 us -> none  [shards(): lax.all_to_all(flat_out, ('task', 'shard'), split_axis=0, concat_axis=0,...]
    all_to_all x1 -> x0, starting transfers between devices: 5.72 us -> none  [shards(): lax.all_to_all(flat_out, ('task', 'shard'), split_axis=0, concat_axis=0,...]
    unnamed x11 -> x2, local copies, waits for them, and re-layouts: 0.18 us -> 3.97 us
    all_gather x1 -> x0, local copies, waits for them, and re-layouts: 2.31 us -> none  [shards(): copies = lax.all_gather(result, 'rep', axis=3, tiled=True)]
    gather x7 -> x0, local copies, waits for them, and re-layouts: 2.16 us -> none  [the longest x6 1.57 us: slot_blocks(): jnp.take_along_axis(sel_index, where_at.reshape(sel_index.shape[0], -1),...]
  transfers between devices with their start and end apart: 2 -> 0, of which waited for: 2 -> 0; matrix products, arithmetic and copies ran while one was open for 3% -> 0% of each run, Pallas kernels for 0% -> 0%
where the time goes in v1:
time: 40.1 us; the launch traced here: 39.9 us
  Pallas kernels  35.9 us (90%)
  local copies, waits for them, and re-layouts  3.97 us (10%)
    pallas_call x1, Pallas kernels, shards(): pl.pallas_call(functools.partial(kernel, dims), out_shape=jax.ShapeDtypeS...  35.9 us
    unnamed x2, local copies, waits for them, and re-layouts  3.97 us

profile of v1, /device:TPU:9, one launch (start us, length us, event | category | flops | bytes accessed | tf_op | source)
XLA Modules:
  0.0 39.9 jit_solution(12177962347015301696)
XLA Ops:
  0.0 1.7 %copy.8 = bf16[4,16,2,1024]{3,1,2,0:T(8,128)(2,1)} copy(bf16[4,16,2,1024]{3,2,1,0:T(2,128)(2,1)} %param.6) | data formatting | bytes 524288 | tf_op args[1]
  1.7 35.9 %shard_map.55 = bf16[4,16,8192]{2,1,0:T(8,128)(2,1)} custom-call(s32[8,8]{1,0:T(8,128)} %index_ref.1, s32[8]{0:T(128)} %count_ref.1, s32[8]{0:T(128)} %scale_ref.1, bf16[2,32,16,1024]{3,2,1,0:T(8,128)(2,1)} %deltas_ref.1, bf16[4,2,16,1024]{3,2,1,0:T(8,128)(2,1)} %bitcast.3), custom_call_target="tpu_custom_call" | custom-call | tf_op jit(solution)/shard_map/pallas_call | solution.py:205
  37.6 2.3 %copy.10 = bf16[4,16,8192]{2,1,0:T(8,128)(2,1)} copy(bf16[4,16,8192]{2,1,0:T(8,128)(2,1)} %shard_map.55) | data formatting | bytes 2097152

commit v2 on v1

--- a/solution.py
+++ b/solution.py
@@ -16,15 +16,18 @@
 
 
 def offset_peers(n_task, n_shard, n_rep, layer_tasks):
-    owners = [(a, b) for a in range(n_task) for b in range(n_shard)][1:]
+    order = sorted(range(n_task), key=lambda a: (-min(a, n_task - a), -a))
+    owners = [(a, b) for a in order for b in range(n_shard) if a or b]
     group = [(a, b, c) for a in range(layer_tasks) for b in range(n_shard) for c in range(n_rep)][1:]
     return owners, group
 
 
 def kernel(
-    dims, index_ref, count_ref, scale_ref, deltas_ref, base_ref, out_ref,
-    held, base_held, outgoing, incoming, raw, stat_mine, stat_in,
-    load_sems, base_sem, send_sems, recv_sems, stat_send, stat_recv, col_send, col_recv,
+    dims, index_hbm, count_hbm, scale_hbm, deltas_ref, base_ref, out_ref,
+    index_ref, count_ref, scale_ref,
+    held, base_held, outgoing, incoming, raw, mine, stat_mine, stat_in,
+    table_sems, load_sems, base_sem, send_sems, recv_sems, stat_send, stat_recv,
+    far_send, far_recv, near_send, near_recv, pass_send, pass_recv, keep_sems,
 ):
     n_task, n_shard, n_rep, layer_tasks = dims
     task_dev, nb_all, rows, width = deltas_ref.shape
@@ -37,6 +40,13 @@
     my_shard = lax.axis_index("shard")
     my_rep = lax.axis_index("rep")
 
+    tables = []
+    for i, (src, dst) in enumerate(
+        ((index_hbm, index_ref), (count_hbm, count_ref), (scale_hbm, scale_ref))
+    ):
+        copy = pltpu.make_async_copy(src, dst, table_sems.at[i])
+        copy.start()
+        tables.append(copy)
     loads = []
     for a in range(task_dev):
         copy = pltpu.make_async_copy(deltas_ref.at[a], held.at[a], load_sems.at[a])
@@ -62,9 +72,12 @@
     for off in owner_offsets:
         t, s = owner_at(off)
         pl.semaphore_signal(barrier, inc=1, device_id=(t, s, my_rep), device_id_type=MESH)
-    extra = [o for o in stat_offsets if o[2] != 0 or (o[0] != 0 and n_task % layer_tasks)]
+    extra = [o for o in stat_offsets if o[2] != 0]
     for off in extra:
         pl.semaphore_signal(barrier, inc=1, device_id=stat_at(off), device_id_type=MESH)
+
+    for copy in tables:
+        copy.wait()
 
     def block_for(task, owner):
         count = count_ref[task]
@@ -114,7 +127,7 @@
     base_sum = jnp.zeros((rows, LANES), jnp.float32)
     for g in range(groups):
         for j in range(own_blocks):
-            wide = base_held[j, g].astype(jnp.float32)
+            wide = base_held[j, :, g, :].astype(jnp.float32)
             raw[g, j] = wide
             base_sum = base_sum + fold(wide * wide)
     stat_mine[0] = base_sum
@@ -170,23 +183,51 @@
     merged_total = jnp.sum(merged_total, axis=(0, 1), keepdims=True)
     ratio = jnp.sqrt((base_total + epsilon) / (merged_total + epsilon))
 
-    cols = []
+    pairs = n_rep // 2
+    pair, core = my_rep // 2, lax.rem(my_rep, 2)
+    sibling = (my_task, my_shard, pair * 2 + 1 - core)
+
+    def columns(g, rep):
+        col = pl.multiple_of(g * group_cols + rep * width, width)
+        return out_ref.at[:, :, pl.ds(col, width)]
+
+    far, near, passed, keeps = [], [], [], []
     for g in range(groups):
-        col = pl.multiple_of(g * group_cols + my_rep * width, width)
-        for j in range(own_blocks):
-            out_ref[j, :, pl.ds(col, width)] = (raw[g, j] * ratio).astype(jnp.bfloat16)
-        part = out_ref.at[:, :, pl.ds(col, width)]
-        for c in range(1, n_rep):
+        for j in range(own_blocks):
+            mine[g, j] = (raw[g, j] * ratio).astype(jnp.bfloat16)
+        for k in range(1, pairs):
             copy = pltpu.make_async_remote_copy(
-                src_ref=part, dst_ref=part,
-                send_sem=col_send.at[g, c - 1], recv_sem=col_recv.at[g, c - 1],
-                device_id=(my_task, my_shard, lax.rem(my_rep + c, n_rep)), device_id_type=MESH,
+                src_ref=mine.at[g], dst_ref=columns(g, my_rep),
+                send_sem=far_send.at[g, k - 1], recv_sem=far_recv.at[g, k - 1],
+                device_id=(my_task, my_shard, lax.rem(pair + k, pairs) * 2 + core), device_id_type=MESH,
             )
             copy.start()
-            cols.append(copy)
-    for copy in cols:
+            far.append((g, k, copy))
+        copy = pltpu.make_async_remote_copy(
+            src_ref=mine.at[g], dst_ref=columns(g, my_rep),
+            send_sem=near_send.at[g], recv_sem=near_recv.at[g],
+            device_id=sibling, device_id_type=MESH,
+        )
+        copy.start()
+        near.append(copy)
+        copy = pltpu.make_async_copy(mine.at[g], columns(g, my_rep), keep_sems.at[g])
+        copy.start()
+        keeps.append(copy)
+    for g, k, copy in far:
         copy.wait_recv()
-    for copy in sends + stats + cols:
+        part = columns(g, lax.rem(pair - k + pairs, pairs) * 2 + core)
+        copy = pltpu.make_async_remote_copy(
+            src_ref=part, dst_ref=part,
+            send_sem=pass_send.at[g, k - 1], recv_sem=pass_recv.at[g, k - 1],
+            device_id=sibling, device_id_type=MESH,
+        )
+        copy.start()
+        passed.append(copy)
+    for copy in near + passed:
+        copy.wait_recv()
+    for copy in keeps:
+        copy.wait()
+    for copy in sends + stats + [c for _, _, c in far] + near + passed:
         copy.wait_send()
 
 
@@ -199,32 +240,40 @@
         layer_tasks = nb_all // LAYERS // own_blocks // n_shard
         dims = (n_task, n_shard, n_rep, layer_tasks)
         peers, group = offset_peers(*dims)
-        smem = pl.BlockSpec(memory_space=pltpu.SMEM)
-        hbm = pl.BlockSpec(memory_space=pl.ANY)
-        base = jnp.transpose(base, (0, 2, 1, 3))
+        hbm = pl.BlockSpec(memory_space=pltpu.HBM)
         return pl.pallas_call(
             functools.partial(kernel, dims),
             out_shape=jax.ShapeDtypeStruct((own_blocks, rows, groups * n_rep * width), jnp.bfloat16),
-            in_specs=[smem, smem, smem, hbm, hbm],
-            out_specs=pl.BlockSpec(memory_space=pltpu.VMEM),
+            in_specs=[hbm] * 5,
+            out_specs=pl.BlockSpec(memory_space=pl.ANY),
             scratch_shapes=[
+                pltpu.SMEM(sel_index.shape, jnp.int32),
+                pltpu.SMEM(sel_count.shape, jnp.int32),
+                pltpu.SMEM(scale_num.shape, jnp.int32),
                 pltpu.VMEM(deltas.shape, jnp.bfloat16),
                 pltpu.VMEM(base.shape, jnp.bfloat16),
                 pltpu.VMEM((len(peers), task_dev, rows, width), jnp.bfloat16),
                 pltpu.VMEM((len(peers), task_dev, rows, width), jnp.bfloat16),
                 pltpu.VMEM((groups, own_blocks, rows, width), jnp.float32),
+                pltpu.VMEM((groups, own_blocks, rows, width), jnp.bfloat16),
                 pltpu.VMEM((2, rows, LANES), jnp.float32),
                 pltpu.VMEM((len(group), 2, rows, LANES), jnp.float32),
+                pltpu.SemaphoreType.DMA((3,)),
                 pltpu.SemaphoreType.DMA((task_dev,)),
                 pltpu.SemaphoreType.DMA,
                 pltpu.SemaphoreType.DMA((len(peers),)),
                 pltpu.SemaphoreType.DMA((len(peers),)),
                 pltpu.SemaphoreType.DMA((len(group),)),
                 pltpu.SemaphoreType.DMA((len(group),)),
-                pltpu.SemaphoreType.DMA((groups, n_rep - 1)),
-                pltpu.SemaphoreType.DMA((groups, n_rep - 1)),
+                pltpu.SemaphoreType.DMA((groups, n_rep // 2)),
+                pltpu.SemaphoreType.DMA((groups, n_rep // 2)),
+                pltpu.SemaphoreType.DMA((groups,)),
+                pltpu.SemaphoreType.DMA((groups,)),
+                pltpu.SemaphoreType.DMA((groups, n_rep // 2)),
+                pltpu.SemaphoreType.DMA((groups, n_rep // 2)),
+                pltpu.SemaphoreType.DMA((groups,)),
             ],
-            compiler_params=pltpu.CompilerParams(collective_id=0, has_side_effects=True),
+            compiler_params=pltpu.CompilerParams(collective_id=0, has_side_effects=True, vmem_limit_bytes=16 * 1024 * 1024),
         )(sel_index, sel_count, scale_num, deltas, base)
 
     placed = (

time: 40.1 us -> 36.4 us (0.908)
  Pallas kernels: 35.9 us -> 30.7 us
  local copies, waits for them, and re-layouts: 3.97 us -> 5.51 us
    pallas_call x1, Pallas kernels: 35.9 us -> 30.7 us  [shards(): pl.pallas_call(functools.partial(kernel, dims), out_shape=jax.ShapeDtypeS...]
    unnamed x2 -> x11, local copies, waits for them, and re-layouts: 3.97 us -> 5.51 us
where the time goes in v2:
time: 36.4 us; the launch traced here: 36.2 us
  Pallas kernels  30.7 us (84%)
  local copies, waits for them, and re-layouts  5.51 us (15%)
    pallas_call x1, Pallas kernels, shards(): pl.pallas_call(functools.partial(kernel, dims), out_shape=jax.ShapeDtypeS...  30.7 us
    unnamed x11, local copies, waits for them, and re-layouts  5.51 us

profile of v2, /device:TPU:9, one launch (start us, length us, event | category | flops | bytes accessed | tf_op | source)
XLA Modules:
  0.0 36.2 jit_solution(8240709542437305632)
XLA Ops:
  0.0 0.0 copy-start
  0.0 1.6 %copy-done = bf16[2,32,16,1024]{3,2,1,0:T(8,128)(2,1)S(1)} copy-done((bf16[2,32,16,1024]{3,2,1,0:T(8,128)(2,1)S(1)}, bf16[2,32,16,1024]{3,2,1,0:T(8,128)(2,1)}, u32[]{:S(2)}) %copy-start) | copy-done | bytes 2097176
  1.6 0.0 copy-start.1
  1.6 0.9 %copy-done.1 = bf16[4,16,2,1024]{3,2,1,0:T(2,128)(2,1)S(1)} copy-done((bf16[4,16,2,1024]{3,2,1,0:T(2,128)(2,1)S(1)}, bf16[4,16,2,1024]{3,2,1,0:T(2,128)(2,1)}, u32[]{:S(2)}) %copy-start.1) | copy-done | bytes 262168
  2.5 0.0 copy-start.2
  2.5 0.7 %copy-done.2 = s32[8,8]{1,0:T(8,128)S(1)} copy-done((s32[8,8]{1,0:T(8,128)S(1)}, s32[8,8]{1,0:T(8,128)}, u32[]{:S(2)}) %copy-start.2) | copy-done | bytes 280
  3.2 0.0 copy-start.3
  3.2 0.7 %copy-done.3 = s32[8]{0:T(128)S(1)} copy-done((s32[8]{0:T(128)S(1)}, s32[8]{0:T(128)}, u32[]{:S(2)}) %copy-start.3) | copy-done | bytes 56
  3.9 0.0 copy-start.4
  3.9 0.7 %copy-done.4 = s32[8]{0:T(128)S(1)} copy-done((s32[8]{0:T(128)S(1)}, s32[8]{0:T(128)}, u32[]{:S(2)}) %copy-start.4) | copy-done | bytes 56
  4.5 30.7 %shard_map.55 = bf16[4,16,8192]{2,1,0:T(8,128)(2,1)S(1)} custom-call(s32[8,8]{1,0:T(8,128)S(1)} %copy-done.2, s32[8]{0:T(128)S(1)} %copy-done.3, s32[8]{0:T(128)S(1)} %copy-done.4, bf16[2,32,16,1024]{3,2,1,0:T(8,128)(2,1)S(1)} %copy-done, bf16[4,16,2,1024]{3,2,1,0:T(2,128)(2,1)S(1)} %copy-done.1), custom_call_target="tpu_custom_call" | custom-call | tf_op jit(solution)/shard_map/pallas_call | solution.py:244
  35.2 1.0 %copy.7 = bf16[4,16,8192]{2,1,0:T(8,128)(2,1)} copy(bf16[4,16,8192]{2,1,0:T(8,128)(2,1)S(1)} %shard_map.55) | data formatting | bytes 2097152
Async XLA Ops:
  0.0 1.6 %copy-start = (bf16[2,32,16,1024]{3,2,1,0:T(8,128)(2,1)S(1)}, bf16[2,32,16,1024]{3,2,1,0:T(8,128)(2,1)}, u32[]{:S(2)}) copy-start(bf16[2,32,16,1024]{3,2,1,0:T(8,128)(2,1)} %deltas_ref.1) | copy-start | bytes 6291460
  1.6 0.9 %copy-start.1 = (bf16[4,16,2,1024]{3,2,1,0:T(2,128)(2,1)S(1)}, bf16[4,16,2,1024]{3,2,1,0:T(2,128)(2,1)}, u32[]{:S(2)}) copy-start(bf16[4,16,2,1024]{3,2,1,0:T(2,128)(2,1)} %base_ref.1) | copy-start | bytes 786436
  2.5 0.7 %copy-start.2 = (s32[8,8]{1,0:T(8,128)S(1)}, s32[8,8]{1,0:T(8,128)}, u32[]{:S(2)}) copy-start(s32[8,8]{1,0:T(8,128)} %index_hbm.1) | copy-start | bytes 772
  3.2 0.7 %copy-start.3 = (s32[8]{0:T(128)S(1)}, s32[8]{0:T(128)}, u32[]{:S(2)}) copy-start(s32[8]{0:T(128)} %count_hbm.1) | copy-start | bytes 100
  3.9 0.7 %copy-start.4 = (s32[8]{0:T(128)S(1)}, s32[8]{0:T(128)}, u32[]{:S(2)}) copy-start(s32[8]{0:T(128)} %scale_hbm.1) | copy-start | bytes 100

commit v3 on v2

--- a/solution.py
+++ b/solution.py
@@ -274,7 +274,7 @@
                 pltpu.SemaphoreType.DMA((groups,)),
             ],
             compiler_params=pltpu.CompilerParams(collective_id=0, has_side_effects=True, vmem_limit_bytes=16 * 1024 * 1024),
-        )(sel_index, sel_count, scale_num, deltas, base)
+        )(*[pltpu.with_memory_space_constraint(x, pltpu.HBM) for x in (sel_index, sel_count, scale_num, deltas, base)])
 
     placed = (
         P("task", None, None, ("shard", "rep")),

time: 36.4 us -> 31.6 us (0.87)
  local copies, waits for them, and re-layouts: 5.51 us -> 0.97 us
    unnamed x11 -> x1, local copies, waits for them, and re-layouts: 5.51 us -> 0.97 us
where the time goes in v3:
time: 31.6 us; the launch traced here: 31.5 us
  Pallas kernels  30.5 us (97%)
  local copies, waits for them, and re-layouts  0.97 us (3%)
    pallas_call x1, Pallas kernels, shards(): pl.pallas_call(functools.partial(kernel, dims), out_shape=jax.ShapeDtypeS...  30.5 us
    unnamed x1, local copies, waits for them, and re-layouts  0.97 us

profile of v3, /device:TPU:9, one launch (start us, length us, event | category | flops | bytes accessed | tf_op | source)
XLA Modules:
  0.0 31.5 jit_solution(654031441736716322)
XLA Ops:
  0.0 30.5 %shard_map.55 = bf16[4,16,8192]{2,1,0:T(8,128)(2,1)S(1)} custom-call(s32[8,8]{1,0:T(8,128)} %index_hbm.1, s32[8]{0:T(128)} %count_hbm.1, s32[8]{0:T(128)} %scale_hbm.1, bf16[2,32,16,1024]{3,2,1,0:T(8,128)(2,1)} %deltas_ref.1, bf16[4,16,2,1024]{3,2,1,0:T(2,128)(2,1)} %base_ref.1), custom_call_target="tpu_custom_call" | custom-call | tf_op jit(solution)/shard_map/pallas_call | solution.py:244
  30.5 1.0 %copy.7 = bf16[4,16,8192]{2,1,0:T(8,128)(2,1)} copy(bf16[4,16,8192]{2,1,0:T(8,128)(2,1)S(1)} %shard_map.55) | data formatting | bytes 2097152

commit v4 on v3

v4 whole, which is shorter than its diff:
```python
import functools

import jax
import jax.numpy as jnp
from jax import lax
from jax.experimental import pallas as pl
from jax.experimental.pallas import tpu as pltpu
from jax.sharding import PartitionSpec as P

LAYERS = 4
LANES = 128
EARLY = 5
MESH = pl.DeviceIdType.MESH

denominator = 8.0
epsilon = 1e-06


def offset_peers(n_task, n_shard, n_rep, layer_tasks):
    order = sorted(range(n_task), key=lambda a: (-min(a, n_task - a), -a))
    owners = [(a, b) for a in order for b in range(n_shard) if a or b]
    group = [(a, b, c) for a in range(layer_tasks) for b in range(n_shard) for c in range(n_rep)][1:]
    return owners, group


def kernel(
    dims, index_hbm, count_hbm, scale_hbm, deltas_ref, base_ref, out_ref,
    index_ref, count_ref, scale_ref,
    held, base_held, outgoing, incoming, raw, mine, stat_mine, stat_in,
    own, twin_base, twin_in, twin_raw, twin_mine, twin_send, twin_recv, side_send, side_recv, side_keep,
    table_sems, load_sems, base_sem, send_sems, recv_sems, stat_send, stat_recv,
    far_send, far_recv, near_send, near_recv, pass_send, pass_recv, keep_sems,
):
    n_task, n_shard, n_rep, layer_tasks = dims
    task_dev, nb_all, rows, width = deltas_ref.shape
    groups, own_blocks = raw.shape[:2]
    group_cols = out_ref.shape[2] // groups
    kmax = index_ref.shape[1]
    owner_offsets, stat_offsets = offset_peers(n_task, n_shard, n_rep, layer_tasks)

    my_task = lax.axis_index("task")
    my_shard = lax.axis_index("shard")
    my_rep = lax.axis_index("rep")

    def owner_at(off, sign=1):
        t = lax.rem(my_task + sign * off[0] + n_task, n_task)
        s = lax.rem(my_shard + sign * off[1] + n_shard, n_shard)
        return t, s

    layer_first = (my_task // layer_tasks) * layer_tasks

    def stat_at(off):
        t = layer_first + lax.rem(my_task - layer_first + off[0], layer_tasks)
        s = lax.rem(my_shard + off[1], n_shard)
        r = lax.rem(my_rep + off[2], n_rep)
        return t, s, r

    barrier = pltpu.get_barrier_semaphore()
    for off in owner_offsets:
        t, s = owner_at(off)
        pl.semaphore_signal(barrier, inc=1, device_id=(t, s, my_rep), device_id_type=MESH)
    extra = [o for o in stat_offsets if o[2] != 0]
    for off in extra:
        pl.semaphore_signal(barrier, inc=1, device_id=stat_at(off), device_id_type=MESH)

    tables = []
    for i, (src, dst) in enumerate(
        ((index_hbm, index_ref), (count_hbm, count_ref), (scale_hbm, scale_ref))
    ):
        copy = pltpu.make_async_copy(src, dst, table_sems.at[i])
        copy.start()
        tables.append(copy)
    loads = []
    for a in range(task_dev):
        copy = pltpu.make_async_copy(deltas_ref.at[a], held.at[a], load_sems.at[a])
        copy.start()
        loads.append(copy)
    base_copy = pltpu.make_async_copy(base_ref, base_held, base_sem)
    base_copy.start()

    for copy in tables:
        copy.wait()

    def block_for(task, wanted):
        count = count_ref[task]

        def step(k, carry):
            entry = index_ref[task, k]
            owner = jnp.where(k < count, lax.div(entry, own_blocks), -1)
            return tuple(
                (jnp.where(owner == o, entry, block), jnp.where(owner == o, 1, live))
                for o, (block, live) in zip(wanted, carry)
            )

        start = tuple((o * own_blocks, jnp.int32(0)) for o in wanted)
        if kmax > 8:
            return lax.fori_loop(0, kmax, step, start)
        for k in range(kmax):
            start = step(k, start)
        return start

    slots = [(0, 0)] + owner_offsets
    wanted = []
    for off in slots:
        t, s = owner_at(off)
        wanted.append(t * n_shard + s)
    chosen = {}
    for a in range(task_dev):
        for d, (block, _) in enumerate(block_for(my_task * task_dev + a, wanted)):
            chosen[d, a] = block

    for copy in loads:
        copy.wait()

    for d, off in enumerate(owner_offsets):
        for a in range(task_dev):
            outgoing[d, a] = held[a, chosen[d + 1, a]]
    for a in range(task_dev):
        own[a] = held[a, chosen[0, a]][:, :own.shape[2]]

    pl.semaphore_wait(barrier, len(owner_offsets) + len(extra))

    sends = []
    for d, off in enumerate(owner_offsets):
        t, s = owner_at(off)
        copy = pltpu.make_async_remote_copy(
            src_ref=outgoing.at[d], dst_ref=incoming.at[d],
            send_sem=send_sems.at[d], recv_sem=recv_sems.at[d],
            device_id=(t, s, my_rep), device_id_type=MESH,
        )
        copy.start()
        sends.append(copy)

    pairs = n_rep // 2
    pair, core = my_rep // 2, lax.rem(my_rep, 2)
    twin_rep = lax.rem(pair + 1, pairs) * 2 + core
    early = twin_raw.shape[3]

    def to_twin(i, src, dst):
        copy = pltpu.make_async_remote_copy(
            src_ref=src, dst_ref=dst, send_sem=twin_send.at[i], recv_sem=twin_recv.at[i],
            device_id=(my_task, my_shard, twin_rep), device_id_type=MESH,
        )
        copy.start()
        return copy

    twin_base_copy = to_twin(len(slots), base_ref.at[:, :, :, pl.ds(0, early)], twin_base)
    twins = [to_twin(0, own, twin_in.at[0])]

    def fold(values):
        total = values[:, 0:LANES]
        for c in range(LANES, values.shape[1], LANES):
            total = total + values[:, c:c + LANES]
        return total

    base_copy.wait()
    base_sum = jnp.zeros((rows, LANES), jnp.float32)
    for g in range(groups):
        for j in range(own_blocks):
            wide = base_held[j, :, g, :].astype(jnp.float32)
            raw[g, j] = wide
            base_sum = base_sum + fold(wide * wide)
    stat_mine[0:1] = jnp.sum(base_sum, axis=0, keepdims=True)

    my_owner = my_task * n_shard + my_shard

    weights, sources = [], []
    for off in slots:
        t, s = owner_at(off, -1)
        sources.append(s)
        weights.append([])
        for a in range(task_dev):
            task = t * task_dev + a
            block, live = block_for(task, [my_owner])[0]
            factor = scale_ref[task].astype(jnp.float32) / denominator
            factor = jnp.where(live == 1, factor, 0.0)
            local = block - my_owner * own_blocks
            weights[-1].append([jnp.where(local == j, factor, 0.0) for j in range(own_blocks)])

    def add_in(total_ref, d, pieces):
        pieces = [p.astype(jnp.float32) for p in pieces]
        for j in range(own_blocks):
            total = total_ref[sources[d], j]
            for a in range(task_dev):
                total = total + weights[d][a][j] * pieces[a]
            total_ref[sources[d], j] = total

    def widen_twin():
        twin_base_copy.wait_recv()
        for g in range(groups):
            for j in range(own_blocks):
                twin_raw[g, j] = twin_base[j, :, g, :].astype(jnp.float32)

    def add_twin(i, d):
        twins[i].wait_recv()
        add_in(twin_raw, d, [twin_in[d, a] for a in range(task_dev)])

    add_in(raw, 0, [held[a, chosen[0, a]] for a in range(task_dev)])
    last = len(slots) - 1
    arrivals = [last] + list(range(1, last))
    order = [0] + arrivals
    lag = 3
    for i, d in enumerate(arrivals):
        sends[d - 1].wait_recv()
        twins.append(to_twin(d, incoming.at[d - 1, :, :, pl.ds(0, early)], twin_in.at[d]))
        add_in(raw, d, [incoming[d - 1, a] for a in range(task_dev)])
        if i == lag - 1:
            widen_twin()
        if i >= lag:
            add_twin(i - lag, order[i - lag])

    merged_sum = jnp.zeros((rows, LANES), jnp.float32)
    for g in range(groups):
        for j in range(own_blocks):
            value = raw[g, j]
            merged_sum = merged_sum + fold(value * value)
    stat_mine[1:2] = jnp.sum(merged_sum, axis=0, keepdims=True)

    stats = []
    for e, off in enumerate(stat_offsets):
        copy = pltpu.make_async_remote_copy(
            src_ref=stat_mine, dst_ref=stat_in.at[e],
            send_sem=stat_send.at[e], recv_sem=stat_recv.at[e],
            device_id=stat_at(off), device_id_type=MESH,
        )
        copy.start()
        stats.append(copy)
    for i in range(len(arrivals) - lag, len(order)):
        add_twin(i, order[i])
    totals = stat_mine[...]
    for e in range(len(stat_offsets)):
        stats[e].wait_recv()
        totals = totals + stat_in[e]
    totals = jnp.sum(totals, axis=1, keepdims=True)
    base_total, merged_total = totals[0:1], totals[1:2]
    ratio = jnp.sqrt((base_total + epsilon) / (merged_total + epsilon))

    def columns(g, rep, first, size):
        col = pl.multiple_of(g * group_cols + rep * width + first, LANES)
        return out_ref.at[:, :, pl.ds(col, size)]

    def scaled(ref, g, j, first, size):
        return (ref[g, j, :, pl.ds(first, size)] * ratio).astype(jnp.bfloat16)

    def to_core(src, dst, send, recv, rep):
        copy = pltpu.make_async_remote_copy(
            src_ref=src, dst_ref=dst, send_sem=send, recv_sem=recv,
            device_id=(my_task, my_shard, rep), device_id_type=MESH,
        )
        copy.start()
        return copy

    sibling_rep = pair * 2 + 1 - core
    late = width - early
    far, near, keeps = [], [], []
    for g in range(groups):
        for j in range(own_blocks):
            mine[g, j, :, pl.ds(early, late)] = scaled(raw, g, j, early, late)
        far.append(to_core(
            mine.at[g, :, :, pl.ds(early, late)], columns(g, my_rep, early, late),
            far_send.at[g], far_recv.at[g], twin_rep,
        ))
    for g in range(groups):
        for j in range(own_blocks):
            mine[g, j, :, pl.ds(0, early)] = scaled(raw, g, j, 0, early)
            twin_mine[g, j] = scaled(twin_raw, g, j, 0, early)
        part = columns(g, my_rep, 0, width)
        near.append(to_core(mine.at[g], part, near_send.at[g], near_recv.at[g], sibling_rep))
        keeps.append(pltpu.make_async_copy(mine.at[g], part, keep_sems.at[g]))
        keeps[-1].start()
        part = columns(g, twin_rep, 0, early)
        near.append(to_core(twin_mine.at[g], part, side_send.at[g], side_recv.at[g], sibling_rep))
        keeps.append(pltpu.make_async_copy(twin_mine.at[g], part, side_keep.at[g]))
        keeps[-1].start()
    passed = []
    for g in range(groups):
        far[g].wait_recv()
        part = columns(g, twin_rep, early, late)
        passed.append(to_core(part, part, pass_send.at[g], pass_recv.at[g], sibling_rep))
    for copy in near + passed:
        copy.wait_recv()
    for copy in keeps:
        copy.wait()
    for copy in sends + twins + [twin_base_copy] + stats + far + near + passed:
        copy.wait_send()


def solution(mesh):
    n_task, n_shard, n_rep = mesh.shape["task"], mesh.shape["shard"], mesh.shape["rep"]

    def shards(deltas, base, sel_index, sel_count, scale_num):
        task_dev, nb_all, rows, width = deltas.shape
        own_blocks, _, groups, _ = base.shape
        layer_tasks = nb_all // LAYERS // own_blocks // n_shard
        dims = (n_task, n_shard, n_rep, layer_tasks)
        peers, group = offset_peers(*dims)
        early = width * EARLY // 8 // LANES * LANES
        hbm = pl.BlockSpec(memory_space=pltpu.HBM)
        return pl.pallas_call(
            functools.partial(kernel, dims),
            out_shape=jax.ShapeDtypeStruct((own_blocks, rows, groups * n_rep * width), jnp.bfloat16),
            in_specs=[hbm] * 5,
            out_specs=pl.BlockSpec(memory_space=pl.ANY),
            scratch_shapes=[
                pltpu.SMEM(sel_index.shape, jnp.int32),
                pltpu.SMEM(sel_count.shape, jnp.int32),
                pltpu.SMEM(scale_num.shape, jnp.int32),
                pltpu.VMEM(deltas.shape, jnp.bfloat16),
                pltpu.VMEM(base.shape, jnp.bfloat16),
                pltpu.VMEM((len(peers), task_dev, rows, width), jnp.bfloat16),
                pltpu.VMEM((len(peers), task_dev, rows, width), jnp.bfloat16),
                pltpu.VMEM((groups, own_blocks, rows, width), jnp.float32),
                pltpu.VMEM((groups, own_blocks, rows, width), jnp.bfloat16),
                pltpu.VMEM((2, LANES), jnp.float32),
                pltpu.VMEM((len(group), 2, LANES), jnp.float32),
                pltpu.VMEM((task_dev, rows, early), jnp.bfloat16),
                pltpu.VMEM((own_blocks, rows, groups, early), jnp.bfloat16),
                pltpu.VMEM((len(peers) + 1, task_dev, rows, early), jnp.bfloat16),
                pltpu.VMEM((groups, own_blocks, rows, early), jnp.float32),
                pltpu.VMEM((groups, own_blocks, rows, early), jnp.bfloat16),
                pltpu.SemaphoreType.DMA((len(peers) + 2,)),
                pltpu.SemaphoreType.DMA((len(peers) + 2,)),
                pltpu.SemaphoreType.DMA((groups,)),
                pltpu.SemaphoreType.DMA((groups,)),
                pltpu.SemaphoreType.DMA((groups,)),
                pltpu.SemaphoreType.DMA((3,)),
                pltpu.SemaphoreType.DMA((task_dev,)),
                pltpu.SemaphoreType.DMA,
                pltpu.SemaphoreType.DMA((len(peers),)),
                pltpu.SemaphoreType.DMA((len(peers),)),
                pltpu.SemaphoreType.DMA((len(group),)),
                pltpu.SemaphoreType.DMA((len(group),)),
                pltpu.SemaphoreType.DMA((groups,)),
                pltpu.SemaphoreType.DMA((groups,)),
                pltpu.SemaphoreType.DMA((groups,)),
                pltpu.SemaphoreType.DMA((groups,)),
                pltpu.SemaphoreType.DMA((groups,)),
                pltpu.SemaphoreType.DMA((groups,)),
                pltpu.SemaphoreType.DMA((groups,)),
            ],
            compiler_params=pltpu.CompilerParams(collective_id=0, has_side_effects=True, vmem_limit_bytes=16 * 1024 * 1024),
        )(*[pltpu.with_memory_space_constraint(x, pltpu.HBM) for x in (sel_index, sel_count, scale_num, deltas, base)])

    placed = (
        P("task", None, None, ("shard", "rep")),
        P(("task", "shard"), None, None, "rep"),
        P(),
        P(),
        P(),
    )
    return jax.shard_map(
        shards,
        mesh=mesh,
        in_specs=placed,
        out_specs=P(("task", "shard"), None, None),
        check_vma=False,
    )
```

time: 31.6 us -> 28.7 us (0.908)
  Pallas kernels: 30.5 us -> 27.5 us
    pallas_call x1, Pallas kernels: 30.5 us -> 27.5 us  [shards(): pl.pallas_call(functools.partial(kernel, dims), out_shape=jax.ShapeDtypeS...]
where the time goes in v4:
time: 28.7 us; the launch traced here: 28.5 us
  Pallas kernels  27.5 us (96%)
  local copies, waits for them, and re-layouts  0.97 us (3%)
    pallas_call x1, Pallas kernels, shards(): pl.pallas_call(functools.partial(kernel, dims), out_shape=jax.ShapeDtypeS...  27.5 us
    unnamed x1, local copies, waits for them, and re-layouts  0.97 us

profile of v4, /device:TPU:9, one launch (start us, length us, event | category | flops | bytes accessed | tf_op | source)
XLA Modules:
  0.0 28.5 jit_solution(3726715812857289463)
XLA Ops:
  0.0 27.5 %shard_map.55 = bf16[4,16,8192]{2,1,0:T(8,128)(2,1)S(1)} custom-call(s32[8,8]{1,0:T(8,128)} %index_hbm.1, s32[8]{0:T(128)} %count_hbm.1, s32[8]{0:T(128)} %scale_hbm.1, bf16[2,32,16,1024]{3,2,1,0:T(8,128)(2,1)} %deltas_ref.1, bf16[4,16,2,1024]{3,2,1,0:T(2,128)(2,1)} %base_ref.1), custom_call_target="tpu_custom_call" | custom-call | tf_op jit(solution)/shard_map/pallas_call | solution.py:299
  27.6 1.0 %copy.7 = bf16[4,16,8192]{2,1,0:T(8,128)(2,1)} copy(bf16[4,16,8192]{2,1,0:T(8,128)(2,1)S(1)} %shard_map.55) | data formatting | bytes 2097152

commit v5 on v4

--- a/solution.py
+++ b/solution.py
@@ -9,7 +9,7 @@
 
 LAYERS = 4
 LANES = 128
-EARLY = 5
+EARLY = 6
 MESH = pl.DeviceIdType.MESH
 
 denominator = 8.0
@@ -18,7 +18,7 @@
 
 def offset_peers(n_task, n_shard, n_rep, layer_tasks):
     order = sorted(range(n_task), key=lambda a: (-min(a, n_task - a), -a))
-    owners = [(a, b) for a in order for b in range(n_shard) if a or b]
+    owners = [(a, b) for a in order for b in reversed(range(n_shard)) if a or b]
     group = [(a, b, c) for a in range(layer_tasks) for b in range(n_shard) for c in range(n_rep)][1:]
     return owners, group
 

time: 28.7 us -> 28.1 us (0.979)
  Pallas kernels: 27.5 us -> 26.9 us
    pallas_call x1, Pallas kernels: 27.5 us -> 26.9 us  [shards(): pl.pallas_call(functools.partial(kernel, dims), out_shape=jax.ShapeDtypeS...]
where the time goes in v5:
time: 28.1 us; the launch traced here: 27.9 us
  Pallas kernels  26.9 us (96%)
  local copies, waits for them, and re-layouts  0.97 us (3%)
    pallas_call x1, Pallas kernels, shards(): pl.pallas_call(functools.partial(kernel, dims), out_shape=jax.ShapeDtypeS...  26.9 us
    unnamed x1, local copies, waits for them, and re-layouts  0.97 us

profile of v5, /device:TPU:9, one launch (start us, length us, event | category | flops | bytes accessed | tf_op | source)
XLA Modules:
  0.0 27.9 jit_solution(8797593709314664419)
XLA Ops:
  0.0 26.9 %shard_map.55 = bf16[4,16,8192]{2,1,0:T(8,128)(2,1)S(1)} custom-call(s32[8,8]{1,0:T(8,128)} %index_hbm.1, s32[8]{0:T(128)} %count_hbm.1, s32[8]{0:T(128)} %scale_hbm.1, bf16[2,32,16,1024]{3,2,1,0:T(8,128)(2,1)} %deltas_ref.1, bf16[4,16,2,1024]{3,2,1,0:T(2,128)(2,1)} %base_ref.1), custom_call_target="tpu_custom_call" | custom-call | tf_op jit(solution)/shard_map/pallas_call | solution.py:299
  27.0 1.0 %copy.7 = bf16[4,16,8192]{2,1,0:T(8,128)(2,1)} copy(bf16[4,16,8192]{2,1,0:T(8,128)(2,1)S(1)} %shard_map.55) | data formatting | bytes 2097152
